TPU v7x, 32 devices: a whole 2x2x4 slice. The times are simulated.
32 devices in a mesh: dp: 4 (over y, core), expert: 8 (over z, x).
Axes of the slice: x: 2, y: 2, z: 4, core: 2. Of those that a mesh axis runs over, the one named last changes fastest.
Arguments:
- hidden_in: bfloat16 [2048, 2048], P(('dp', 'expert')), may hold values from -6 to 6
- context: bfloat16 [2048, 2048], P(('dp', 'expert')), may hold values from -6 to 6
- out_proj: bfloat16 [2048, 2048], P(('dp', 'expert')), may hold values from -0.125 to 0.125
- norm_gain: float32 [2048], replicated, may hold values from 0.5 to 1.5
- router: bfloat16 [2048, 64], P(('dp', 'expert')), may hold values from -0.25 to 0.25
- expert_ids: int32 [2048, 8], P(('dp', 'expert')), may hold values from 0 to 63, as said below
- replica_expert: int32 [128], replicated, may hold values from 0 to 63, as said below
- split_pick: int32 [2048, 8], P(('dp', 'expert')), may hold values from 0 to 65535
- up_gate: bfloat16 [128, 2048, 2048], P(('dp', 'expert')), may hold values from -0.125 to 0.125
- down: bfloat16 [128, 1024, 2048], P(('dp', 'expert')), may hold values from -0.1875 to 0.1875
Outputs:
- layer_out: bfloat16 [2048, 2048], P(('dp', 'expert'))
Inputs may be any that keep to these rules, and one draw needn't show every extreme that they name: `expert_ids`: each row names 8 different experts. `replica_expert`: every expert is served by one replica or more.
All inputs are finite; a program needn't handle non-finite values.
Results may differ from a plain program's by a relative error of at most 0.004.
Values may be sent and summed in bfloat16 or wider, within the bound.
A program may use at most 128 MiB of HBM per device.

v0:
```python
import jax
import jax.numpy as jnp
from jax import lax
from jax.sharding import PartitionSpec as P


def rms_norm(residual, norm_gain):
    scale_back = lax.rsqrt(jnp.mean(residual * residual, axis=-1, keepdims=True) + 1e-05)
    return (residual * scale_back * norm_gain).astype(jnp.bfloat16)


def route_block(expert_ids, split_pick, replica_expert):
    replica_total = replica_expert.shape[0]
    replica_iota = lax.iota(jnp.int32, replica_total)
    same_expert = replica_expert[:, None] == replica_expert[None, :]
    earlier = replica_iota[:, None] > replica_iota[None, :]
    replica_rank = jnp.sum((same_expert & earlier).astype(jnp.int32), axis=1)
    serves = expert_ids[:, :, None] == replica_expert[None, None, :]
    replica_count = jnp.sum(serves.astype(jnp.int32), axis=-1)
    wanted = split_pick % replica_count
    matches = serves & (replica_rank[None, None, :] == wanted[:, :, None])
    replica = jnp.sum(jnp.where(matches, replica_iota[None, None, :], 0), axis=-1)
    flat_replica = replica.reshape(-1)
    pair_iota = lax.iota(jnp.int32, flat_replica.shape[0])
    same_target = flat_replica[:, None] == flat_replica[None, :]
    before = pair_iota[:, None] > pair_iota[None, :]
    slot_index = jnp.sum((same_target & before).astype(jnp.int32), axis=1)
    return (replica, slot_index.reshape(replica.shape))


def apply_experts(incoming, up_gate, down, capacity):
    arrived_shape = incoming.shape
    local_reps = up_gate.shape[0]
    hidden_units = down.shape[1]
    stacked = incoming.reshape(-1, local_reps, capacity, incoming.shape[-1])
    gate_up = jnp.einsum("sjcd,jdf->sjcf", stacked, up_gate, preferred_element_type=jnp.float32)
    hidden_act = (jax.nn.silu(gate_up[..., :hidden_units]) * gate_up[..., hidden_units:]).astype(
        jnp.bfloat16
    )
    expert_out = jnp.einsum("sjcf,jfd->sjcd", hidden_act, down, preferred_element_type=jnp.float32)
    return expert_out.astype(jnp.bfloat16).reshape(arrived_shape)


def per_device(
    hidden_in,
    context,
    out_proj,
    norm_gain,
    router,
    expert_ids,
    replica_expert,
    split_pick,
    up_gate,
    down,
):
    tok_rows, model_width = hidden_in.shape
    top_count = expert_ids.shape[1]
    replica_total = replica_expert.shape[0]
    local_reps = up_gate.shape[0]
    data_groups = lax.axis_size("dp")
    expert_groups = lax.axis_size("expert")
    capacity = max(2, 2 * tok_rows * top_count // replica_total)
    summed = jnp.dot(
        context,
        lax.all_gather(out_proj, ("dp", "expert"), axis=0, tiled=True),
        preferred_element_type=jnp.float32,
    )
    router_rows = lax.all_gather(router, ("dp", "expert"), axis=0, tiled=True)
    residual = hidden_in.astype(jnp.float32) + summed
    normed = rms_norm(residual, norm_gain)
    logits = jnp.dot(normed, router_rows, preferred_element_type=jnp.float32)
    hit_mask = expert_ids[:, :, None] == lax.iota(jnp.int32, logits.shape[1])[None, None, :]
    chosen = jnp.sum(jnp.where(hit_mask, logits[:, None, :], 0.0), axis=-1)
    raised = jnp.exp(chosen)
    route_weight = raised / jnp.sum(raised, axis=-1, keepdims=True)
    replica, slot_index = route_block(expert_ids, split_pick, replica_expert)
    within_cap = slot_index < capacity
    buffer_row = jnp.where(within_cap, replica * capacity + slot_index, -1).reshape(-1)
    slot_total = replica_total * capacity
    matches = buffer_row[None, :] == lax.iota(jnp.int32, slot_total)[:, None]
    filled = jnp.any(matches, axis=1)
    row_of_pair = lax.iota(jnp.int32, tok_rows * top_count) // top_count
    anchor = jnp.sum(jnp.where(matches, row_of_pair[None, :], 0), axis=1)
    outgoing = jnp.where(filled[:, None], normed[anchor], jnp.zeros((), jnp.bfloat16))
    outgoing = outgoing.reshape(data_groups, expert_groups, local_reps * capacity, model_width)
    incoming = lax.all_to_all(
        lax.all_to_all(outgoing, "expert", split_axis=1, concat_axis=1, tiled=True),
        "dp",
        split_axis=0,
        concat_axis=0,
        tiled=True,
    )
    results = apply_experts(incoming, up_gate, down, capacity)
    returned = lax.all_to_all(
        lax.all_to_all(results, "dp", split_axis=0, concat_axis=0, tiled=True),
        "expert",
        split_axis=1,
        concat_axis=1,
        tiled=True,
    )
    returned = returned.reshape(slot_total, model_width)
    safe_index = jnp.where(within_cap, replica * capacity + slot_index, 0)
    gathered = returned[safe_index]
    kept_weight = jnp.where(within_cap, route_weight, 0.0)
    layer_out = residual + jnp.sum(kept_weight[:, :, None] * gathered.astype(jnp.float32), axis=1)
    return layer_out.astype(jnp.bfloat16)


def solution(mesh):
    return jax.shard_map(
        per_device,
        mesh=mesh,
        in_specs=(
            P(("dp", "expert"), None),
            P(("dp", "expert"), None),
            P(("dp", "expert"), None),
            P(),
            P(("dp", "expert"), None),
            P(("dp", "expert"), None),
            P(),
            P(("dp", "expert"), None),
            P(("dp", "expert"), None, None),
            P(("dp", "expert"), None, None),
        ),
        out_specs=P(("dp", "expert"), None),
        check_vma=False,
    )
```

profile of v0, /device:TPU:0, one launch (start us, length us, event | category | flops | bytes accessed | tf_op | source)
XLA Modules:
  0.0 520.4 jit_solution(7582275169445691453)
XLA Ops:
  6.5 0.7 all-gather.2.cloned.1.call-update
  7.3 0.8 copy.38
  8.0 0.8 copy.39
  8.8 0.9 convert_reduce_fusion.1
  9.7 1.9 fusion.16
  11.6 0.4 add_select_fusion
  12.0 2.0 select_reduce_fusion.2
  14.0 0.3 convert_reduce_fusion
  14.3 0.3 fusion.14
  14.7 0.3 select_reduce_fusion
  15.0 75.5 %all-gather.2.cloned.1.call-done = bf16[2048,2048]{1,0:T(8,128)(2,1)} async-done(((bf16[64,2048]{1,0:T(8,128)(2,1)}), bf16[2048,2048]{1,0:T(8,128)(2,1)}) %all-gather.2.cloned.1.call-update) | async-done | bytes 8388624 | tf_op jit(solution)/shard_map/all_gather | solution.py:65
  90.5 5.1 multiply_reduce_fusion
  95.6 0.1 multiply_convert_fusion
  95.7 6.0 %gather_fusion = bf16[1024,2048]{1,0:T(8,128)(2,1)} fusion(bf16[64,2048]{1,0:T(8,128)(2,1)S(1)} %multiply_convert_fusion, s32[1024]{0:T(1024)S(1)} %broadcast_clamp_fusion), kind=kCustom, calls=%fused_computation | custom fusion | bytes 8392704 | tf_op jit(solution)/shard_map/gather | solution.py:84
  101.7 2.5 copy_select_fusion
  104.2 97.4 %all_to_all.20 = bf16[4,8,32,2048]{3,2,0,1:T(8,128)(2,1)S(1)} all-to-all(bf16[4,8,32,2048]{3,2,0,1:T(8,128)(2,1)S(1)} %copy_select_fusion), channel_id=1, replica_groups=mesh['dp'=4,'expert'=8] {'expert'}, dimensions={1} | all-to-all | bytes 8388608 | tf_op jit(solution)/shard_map/all_to_all | solution.py:87
  201.6 0.6 copy.43
  202.2 51.7 %all_to_all.21 = bf16[4,8,32,2048]{3,2,1,0:T(8,128)(2,1)} all-to-all(bf16[4,8,32,2048]{3,2,1,0:T(8,128)(2,1)S(1)} %copy.43), channel_id=1, replica_groups=mesh['dp'=4,'expert'=8] {'dp'}, dimensions={0} | all-to-all | bytes 8388608 | tf_op jit(solution)/shard_map/all_to_all | solution.py:86
  253.9 18.3 %fusion.4 = f32[32,4,8,2048]{3,2,0,1:T(8,128)} fusion(bf16[4,2048,2048]{2,1,0:T(8,128)(2,1)} %param.18, bf16[32,4,8,2048]{3,2,1,0:T(8,128)(2,1)} %bitcast.39), kind=kOutput, calls=%fused_computation.6 | convolution fusion | flops 8589934592 | bytes 46137344 | tf_op jit(solution)/shard_map/sjcd,jdf->sjcf/dot_general | solution.py:36
  272.1 14.8 %convert_bitcast_fusion = bf16[32,4,8,2048]{3,2,0,1:T(8,128)(2,1)} fusion(bf16[4,1024,2048]{2,1,0:T(8,128)(2,1)} %param.19, f32[32,4,8,2048]{3,2,0,1:T(8,128)} %fusion.4), kind=kOutput, calls=%fused_computation.13 | convolution fusion | flops 4303355904 | bytes 29360128 | tf_op jit(solution)/shard_map/sjcf,jfd->sjcd/dot_general | solution.py:40
  287.0 2.5 copy.45
  289.5 50.7 %all_to_all.22 = bf16[4,8,32,2048]{3,2,1,0:T(8,128)(2,1)S(1)} all-to-all(bf16[4,8,32,2048]{3,2,1,0:T(8,128)(2,1)S(1)} %bitcast.42), channel_id=1, replica_groups=mesh['dp'=4,'expert'=8] {'dp'}, dimensions={0} | all-to-all | bytes 8388608 | tf_op jit(solution)/shard_map/all_to_all | solution.py:95
  340.2 2.3 copy.46
  342.5 4.7 all-to-all-start.3
  347.5 150.8 %all_gather.7 = bf16[2048,64]{1,0:T(8,128)(2,1)S(1)} all-gather(bf16[64,64]{1,0:T(8,128)(2,1)S(1)} %copy-done.2), channel_id=1, replica_groups=mesh['dp'=4,'expert'=8] {'dp','expert'}, dimensions={0}, use_global_device_ids=true | all-gather | bytes 270336 | tf_op jit(solution)/shard_map/all_gather | solution.py:68
  498.3 0.2 fusion.23
  498.6 0.2 select_reduce_fusion.1
  498.8 0.1 exponential_reduce_fusion
  499.0 4.7 copy.47
  503.8 7.2 %gather_fusion.1 = bf16[512,2048]{1,0:T(8,128)(2,1)S(1)} fusion(bf16[1024,2048]{1,0:T(8,128)(2,1)} %bitcast.40, s32[1024]{0:T(1024)S(1)} %pad_clamp_fusion), kind=kCustom, calls=%fused_computation.1 | custom fusion | bytes 4196352 | tf_op jit(solution)/shard_map/gather | solution.py:103
  511.0 1.8 fusion.8
  512.8 0.8 add_convert_fusion
  (24 shorter events, 0.6 us)
Async XLA Ops:
  6.5 84.0 %copy-start = (bf16[64,2048]{1,0:T(8,128)(2,1)S(1)}, bf16[64,2048]{1,0:T(8,128)(2,1)}, u32[]{:S(2)}) copy-start(bf16[64,2048]{1,0:T(8,128)(2,1)} %param.11) | copy-start | bytes 786436
  6.5 84.0 %all-gather.2.cloned.1.call-start = ((), (), s32[]{:S(2)}) async-start(), calls=%async_computation.4 | async-start | bytes 8650752 | tf_op jit(solution)/shard_map/all_gather | solution.py:65
  15.0 80.6 %copy-start.3 = (f32[2048]{0:T(1024)S(1)}, f32[2048]{0:T(1024)}, u32[]{:S(2)}) copy-start(f32[2048]{0:T(1024)} %param.13) | copy-start | bytes 24580
  342.5 5.0 copy-start.2
  342.5 156.5 %all-to-all-start.3 = ((bf16[4,8,32,2048]{3,2,0,1:T(8,128)(2,1)}), bf16[4,8,32,2048]{3,2,0,1:T(8,128)(2,1)}, u32[]{:S(2)}, u32[]{:S(2)}) async-start(bf16[4,8,32,2048]{3,2,0,1:T(8,128)(2,1)} %copy.46), calls=%async_computation.3 | async-start | bytes 8388608 | tf_op jit(solution)/shard_map/all_to_all | solution.py:94
  503.8 9.8 %copy-start.1 = (bf16[64,2048]{1,0:T(8,128)(2,1)S(1)}, bf16[64,2048]{1,0:T(8,128)(2,1)}, u32[]{:S(2)}) copy-start(bf16[64,2048]{1,0:T(8,128)(2,1)} %param.11) | copy-start | bytes 786436
Sparse Core Ops, SparseCore 0:
  10.3 80.1 all-gather.1
where the time goes:
time: 521 us; the launch traced here: 520 us
  blocking collectives  351 us (67%)
  waiting for transfers between devices  76.2 us (15%)
  matrix products  38.4 us (7%)
  local copies, waits for them, and re-layouts  25.3 us (5%)
  between operations  13.6 us (3%)
  other arithmetic  11.6 us (2%)
    all_gather x1, blocking collectives, per_device(): router_rows = lax.all_gather(router, ('dp', 'expert'), axis=0, tiled=True)  151 us
    all_to_all x1, blocking collectives, per_device(): lax.all_to_all(outgoing, 'expert', split_axis=1, concat_axis=1, tiled=True)  97.4 us
    all_gather x1, waiting for transfers between devices, per_device(): lax.all_gather(out_proj, ('dp', 'expert'), axis=0, tiled=True)  75.5 us
    all_to_all x1, blocking collectives, per_device(): lax.all_to_all(lax.all_to_all(outgoing, 'expert', split_axis=1, concat_ax...  51.7 us
    all_to_all x1, blocking collectives, per_device(): lax.all_to_all(results, 'dp', split_axis=0, concat_axis=0, tiled=True)  50.7 us
    dot_general x1, matrix products, apply_experts(): jnp.einsum('sjcd,jdf->sjcf', stacked, up_gate, preferred_element_type=jnp...  18.3 us
    dot_general x1, matrix products, apply_experts(): jnp.einsum('sjcf,jfd->sjcd', hidden_act, down, preferred_element_type=jnp...  14.8 us
  transfers between devices with their start and end apart: 2, of which 1 were waited for; matrix products, arithmetic and copies ran while one was open for 2% of the time, Pallas kernels for 0%

commit v1 on v0

--- a/solution.py
+++ b/solution.py
@@ -2,6 +2,17 @@
 import jax.numpy as jnp
 from jax import lax
 from jax.sharding import PartitionSpec as P
+
+
+def cut_along(x, dim, size):
+    before, after = (x.shape[:dim], x.shape[dim + 1 :])
+    return jnp.moveaxis(x.reshape(*before, size, -1, *after), dim, 0)
+
+
+def in_order(blocks, dim):
+    blocks = jnp.moveaxis(blocks, 0, dim)
+    shape = blocks.shape
+    return blocks.reshape(*shape[:dim], shape[dim] * shape[dim + 1], *shape[dim + 2 :])
 
 
 def rms_norm(residual, norm_gain):
@@ -91,13 +102,17 @@
         tiled=True,
     )
     results = apply_experts(incoming, up_gate, down, capacity)
-    returned = lax.all_to_all(
-        lax.all_to_all(results, "dp", split_axis=0, concat_axis=0, tiled=True),
-        "expert",
-        split_axis=1,
-        concat_axis=1,
-        tiled=True,
-    )
+    x = lax.all_to_all(results, "dp", split_axis=0, concat_axis=0, tiled=True)
+    length, mine = (lax.axis_size("expert"), lax.axis_index("expert"))
+    tiles = cut_along(x, 1, length)
+    gathered_2 = [tiles[mine]]
+    for step in range(1, length):
+        sent = tiles[(mine + step) % length]
+        gathered_2.append(
+            lax.ppermute(sent, "expert", [(i, (i + step) % length) for i in range(length)])
+        )
+    tiles = jnp.stack(gathered_2)[(mine - jnp.arange(length)) % length]
+    returned = in_order(tiles, 1)
     returned = returned.reshape(slot_total, model_width)
     safe_index = jnp.where(within_cap, replica * capacity + slot_index, 0)
     gathered = returned[safe_index]

time: 521 us -> 490 us (0.940)
  blocking collectives: 351 us -> 220 us
  waiting for transfers between devices: 76.2 us -> 141 us
  starting transfers between devices: 4.68 us -> 21.7 us
  local copies, waits for them, and re-layouts: 25.3 us -> 40.5 us
    all_gather x1, blocking collectives: 151 us -> 70.8 us  [per_device(): router_rows = lax.all_gather(router, ('dp', 'expert'), axis=0, tiled=True)]
    ppermute x0 -> x7, waiting for transfers between devices: none -> 64.5 us  [per_device(): lax.ppermute(sent, 'expert', [(i, (i + step) % length) for i in range(len...]
    all_to_all x1 -> x0, blocking collectives: 50.7 us -> none  [per_device(): lax.all_to_all(results, 'dp', split_axis=0, concat_axis=0, tiled=True)]
    ppermute x0 -> x7, starting transfers between devices: none -> 16.7 us  [per_device(): lax.ppermute(sent, 'expert', [(i, (i + step) % length) for i in range(len...]
    unnamed x10 -> x18, local copies, waits for them, and re-layouts: 1.56 us -> 11 us
    all_to_all x2 -> x0, local copies, waits for them, and re-layouts: 7.02 us -> none  [the longest x1 4.75 us: per_device(): lax.all_to_all(lax.all_to_all(results, 'dp', split_axis=0, concat_axis=0,...]
  transfers between devices with their start and end apart: 2 -> 9, of which waited for: 1 -> 5; matrix products, arithmetic and copies ran while one was open for 2% -> 3% of each run, Pallas kernels for 0% -> 0%
where the time goes in v1:
time: 490 us; the launch traced here: 486 us
  blocking collectives  220 us (45%)
  waiting for transfers between devices  141 us (29%)
  local copies, waits for them, and re-layouts  40.5 us (8%)
  matrix products  38.4 us (8%)
  starting transfers between devices  21.7 us (4%)
  between operations  13.8 us (3%)
  other arithmetic  11.7 us (2%)
    all_to_all x1, blocking collectives, per_device(): lax.all_to_all(outgoing, 'expert', split_axis=1, concat_axis=1, tiled=True)  97.4 us
    all_gather x1, waiting for transfers between devices, per_device(): lax.all_gather(out_proj, ('dp', 'expert'), axis=0, tiled=True)  75.5 us
    all_gather x1, blocking collectives, per_device(): router_rows = lax.all_gather(router, ('dp', 'expert'), axis=0, tiled=True)  70.8 us
    ppermute x7, waiting for transfers between devices, per_device(): lax.ppermute(sent, 'expert', [(i, (i + step) % length) for i in range(len...  64.5 us
    all_to_all x1, blocking collectives, per_device(): lax.all_to_all(lax.all_to_all(outgoing, 'expert', split_axis=1, concat_ax...  51.7 us
    dot_general x1, matrix products, apply_experts(): jnp.einsum('sjcd,jdf->sjcf', stacked, up_gate, preferred_element_type=jnp...  18.3 us
    ppermute x7, starting transfers between devices, per_device(): lax.ppermute(sent, 'expert', [(i, (i + step) % length) for i in range(len...  16.7 us
    dot_general x1, matrix products, apply_experts(): jnp.einsum('sjcf,jfd->sjcd', hidden_act, down, preferred_element_type=jnp...  14.8 us
  transfers between devices with their start and end apart: 9, of which 5 were waited for; matrix products, arithmetic and copies ran while one was open for 3% of the time, Pallas kernels for 0%

profile of v1, /device:TPU:0, one launch (start us, length us, event | category | flops | bytes accessed | tf_op | source)
XLA Modules:
  0.0 486.4 jit_solution(17880633017927560534)
XLA Ops:
  8.8 0.9 convert_reduce_fusion.1
  9.7 1.9 fusion.16
  12.0 2.0 select_reduce_fusion.2
  15.0 75.5 %all-gather.2.cloned.1.call-done = bf16[2048,2048]{1,0:T(8,128)(2,1)} async-done(((bf16[64,2048]{1,0:T(8,128)(2,1)}), bf16[2048,2048]{1,0:T(8,128)(2,1)}) %all-gather.2.cloned.1.call-update) | async-done | bytes 8388624 | tf_op jit(solution)/shard_map/all_gather | solution.py:76
  90.5 5.1 %multiply_reduce_fusion = (f32[64]{0:T(128)S(1)}, f32[64,2048]{1,0:T(8,128)S(1)}) fusion(bf16[64,2048]{1,0:T(8,128)(2,1)S(1)} %copy-done, bf16[2048,2048]{1,0:T(8,128)(2,1)} %all-gather.2.cloned.1.call-done, bf16[64,2048]{1,0:T(8,128)(2,1)} %param.10), kind=kOutput, calls=%fused_computation.40 | convolution fusion | flops 537395136 | bytes 9437440 | tf_op jit(solution)/shard_map/dot_general | solution.py:74
  95.7 6.0 %gather_fusion = bf16[1024,2048]{1,0:T(8,128)(2,1)} fusion(bf16[64,2048]{1,0:T(8,128)(2,1)S(1)} %multiply_convert_fusion, s32[1024]{0:T(1024)S(1)} %broadcast_clamp_fusion), kind=kCustom, calls=%fused_computation | custom fusion | bytes 8392704 | tf_op jit(solution)/shard_map/gather | solution.py:95
  101.7 2.5 copy_select_fusion
  104.2 97.4 %all_to_all.15 = bf16[4,8,32,2048]{3,2,0,1:T(8,128)(2,1)S(1)} all-to-all(bf16[4,8,32,2048]{3,2,0,1:T(8,128)(2,1)S(1)} %copy_select_fusion), channel_id=1, replica_groups=mesh['dp'=4,'expert'=8] {'expert'}, dimensions={1} | all-to-all | bytes 8388608 | tf_op jit(solution)/shard_map/all_to_all | solution.py:98
  202.2 51.7 %all_to_all.16 = bf16[4,8,32,2048]{3,2,1,0:T(8,128)(2,1)} all-to-all(bf16[4,8,32,2048]{3,2,1,0:T(8,128)(2,1)S(1)} %copy.81), channel_id=1, replica_groups=mesh['dp'=4,'expert'=8] {'dp'}, dimensions={0} | all-to-all | bytes 8388608 | tf_op jit(solution)/shard_map/all_to_all | solution.py:97
  253.9 18.3 %fusion.4 = f32[32,4,8,2048]{3,2,0,1:T(8,128)} fusion(bf16[4,2048,2048]{2,1,0:T(8,128)(2,1)} %param.18, bf16[32,4,8,2048]{3,2,1,0:T(8,128)(2,1)} %bitcast.75), kind=kOutput, calls=%fused_computation.7 | convolution fusion | flops 8589934592 | bytes 46137344 | tf_op jit(solution)/shard_map/sjcd,jdf->sjcf/dot_general | solution.py:47
  272.1 14.8 %convert_bitcast_fusion = bf16[32,4,8,2048]{3,2,0,1:T(8,128)(2,1)} fusion(bf16[4,1024,2048]{2,1,0:T(8,128)(2,1)} %param.19, f32[32,4,8,2048]{3,2,0,1:T(8,128)} %fusion.4), kind=kOutput, calls=%fused_computation.14 | convolution fusion | flops 4303355904 | bytes 29360128 | tf_op jit(solution)/shard_map/sjcf,jfd->sjcd/dot_general | solution.py:51
  287.0 4.7 copy.83
  291.7 5.0 %all-to-all-start.2 = ((bf16[4,8,32,2048]{3,2,1,0:T(8,128)(2,1)}), bf16[4,8,32,2048]{3,2,1,0:T(8,128)(2,1)}, u32[]{:S(2)}, u32[]{:S(2)}) async-start(bf16[4,8,32,2048]{3,2,1,0:T(8,128)(2,1)} %bitcast.78), calls=%async_computation.2 | async-start | bytes 8388608 | tf_op jit(solution)/shard_map/all_to_all | solution.py:105
  297.2 70.8 %all_gather.7 = bf16[2048,64]{1,0:T(8,128)(2,1)S(1)} all-gather(bf16[64,64]{1,0:T(8,128)(2,1)S(1)} %copy-done.2), channel_id=1, replica_groups=mesh['dp'=4,'expert'=8] {'dp','expert'}, dimensions={0}, use_global_device_ids=true | all-gather | bytes 270336 | tf_op jit(solution)/shard_map/all_gather | solution.py:79
  368.4 2.5 dynamic-slice_bitcast_fusion
  370.9 3.9 collective-permute-start
  375.0 1.0 collective-permute-start.6
  376.0 2.0 collective-permute-start.1
  378.0 1.9 bitcast_dynamic-update-slice_fusion.7
  379.9 11.6 %collective-permute-done = bf16[4,1,32,2048]{3,2,0,1:T(8,128)(2,1)S(1)} collective-permute-done((bf16[4,1,32,2048]{3,2,0,1:T(8,128)(2,1)S(1)}, bf16[4,1,32,2048]{3,2,0,1:T(8,128)(2,1)S(1)}, u32[]{:S(2)}, u32[]{:S(2)}) %collective-permute-start) | collective-permute-done | bytes 524320 | tf_op jit(solution)/shard_map/ppermute | solution.py:112
  392.3 0.9 bitcast_dynamic-update-slice_fusion.6
  393.1 27.7 %collective-permute-done.1 = bf16[4,1,32,2048]{3,2,0,1:T(8,128)(2,1)S(1)} collective-permute-done((bf16[4,1,32,2048]{3,2,0,1:T(8,128)(2,1)S(1)}, bf16[4,1,32,2048]{3,2,0,1:T(8,128)(2,1)S(1)}, u32[]{:S(2)}, u32[]{:S(2)}) %collective-permute-start.1) | collective-permute-done | bytes 524320 | tf_op jit(solution)/shard_map/ppermute | solution.py:112
  420.8 9.0 %collective-permute-start.3 = (bf16[4,1,32,2048]{3,2,0,1:T(8,128)(2,1)S(1)}, bf16[4,1,32,2048]{3,2,0,1:T(8,128)(2,1)S(1)}, u32[]{:S(2)}, u32[]{:S(2)}) collective-permute-start(bf16[4,1,32,2048]{3,2,0,1:T(8,128)(2,1)S(1)} %get-tuple-element.8), channel_id=1, source_target_pairs={{0,4},{1,5},{2,6},{3,7},{4,0},{5,1},{6,2},{7,3},{8,12},{9,13},{10,... | collective-permute-start | bytes 1572872 | tf_op jit(solution)/shard_map/ppermute | solution.py:112
  430.7 18.7 %collective-permute-done.2 = bf16[4,1,32,2048]{3,2,0,1:T(8,128)(2,1)S(1)} collective-permute-done((bf16[4,1,32,2048]{3,2,0,1:T(8,128)(2,1)S(1)}, bf16[4,1,32,2048]{3,2,0,1:T(8,128)(2,1)S(1)}, u32[]{:S(2)}, u32[]{:S(2)}) %collective-permute-start.2) | collective-permute-done | bytes 524320 | tf_op jit(solution)/shard_map/ppermute | solution.py:112
  449.4 0.8 bitcast_dynamic-update-slice_fusion.4
  450.2 6.5 %collective-permute-done.3 = bf16[4,1,32,2048]{3,2,0,1:T(8,128)(2,1)S(1)} collective-permute-done((bf16[4,1,32,2048]{3,2,0,1:T(8,128)(2,1)S(1)}, bf16[4,1,32,2048]{3,2,0,1:T(8,128)(2,1)S(1)}, u32[]{:S(2)}, u32[]{:S(2)}) %collective-permute-start.3) | collective-permute-done | bytes 524320 | tf_op jit(solution)/shard_map/ppermute | solution.py:112
  457.6 0.9 bitcast_dynamic-update-slice_fusion.2
  459.3 0.8 bitcast_dynamic-update-slice_fusion
  460.1 4.9 %gather_fusion.1 = bf16[8,4,32,2048]{3,2,1,0:T(8,128)(2,1)} fusion(bf16[8,4,32,2048]{3,2,1,0:T(8,128)(2,1)} %bitcast.19, s32[1024]{0:T(1024)S(1)} %pad_clamp_fusion.1), kind=kCustom, calls=%fused_computation.1 | custom fusion | bytes 8388640 | tf_op jit(solution)/shard_map/gather | solution.py:114
  465.0 4.7 copy.91
  469.8 7.2 %gather_fusion.2 = bf16[512,2048]{1,0:T(8,128)(2,1)S(1)} fusion(bf16[1024,2048]{1,0:T(8,128)(2,1)} %bitcast.76, s32[1024]{0:T(1024)S(1)} %pad_clamp_fusion), kind=kCustom, calls=%fused_computation.2 | custom fusion | bytes 4196352 | tf_op jit(solution)/shard_map/gather | solution.py:118
  477.0 1.8 fusion.8
  (48 shorter events, 9.5 us)
Async XLA Ops:
  6.5 84.0 %copy-start = (bf16[64,2048]{1,0:T(8,128)(2,1)S(1)}, bf16[64,2048]{1,0:T(8,128)(2,1)}, u32[]{:S(2)}) copy-start(bf16[64,2048]{1,0:T(8,128)(2,1)} %param.11) | copy-start | bytes 786436
  6.5 84.0 %all-gather.2.cloned.1.call-start = ((), (), s32[]{:S(2)}) async-start(), calls=%async_computation.3 | async-start | bytes 8650752 | tf_op jit(solution)/shard_map/all_gather | solution.py:76
  15.0 80.6 %copy-start.3 = (f32[2048]{0:T(1024)S(1)}, f32[2048]{0:T(1024)}, u32[]{:S(2)}) copy-start(f32[2048]{0:T(1024)} %param.13) | copy-start | bytes 24580
  291.7 5.5 %copy-start.2 = (bf16[64,64]{1,0:T(8,128)(2,1)S(1)}, bf16[64,64]{1,0:T(8,128)(2,1)}, u32[]{:S(2)}) copy-start(bf16[64,64]{1,0:T(8,128)(2,1)} %param.14) | copy-start | bytes 24580
  291.7 76.7 %all-to-all-start.2 = ((bf16[4,8,32,2048]{3,2,1,0:T(8,128)(2,1)}), bf16[4,8,32,2048]{3,2,1,0:T(8,128)(2,1)}, u32[]{:S(2)}, u32[]{:S(2)}) async-start(bf16[4,8,32,2048]{3,2,1,0:T(8,128)(2,1)} %bitcast.78), calls=%async_computation.2 | async-start | bytes 8388608 | tf_op jit(solution)/shard_map/all_to_all | solution.py:105
  370.9 20.5 %collective-permute-start = (bf16[4,1,32,2048]{3,2,0,1:T(8,128)(2,1)S(1)}, bf16[4,1,32,2048]{3,2,0,1:T(8,128)(2,1)S(1)}, u32[]{:S(2)}, u32[]{:S(2)}) collective-permute-start(bf16[4,1,32,2048]{3,2,0,1:T(8,128)(2,1)S(1)} %get-tuple-element.11), channel_id=1, source_target_pairs={{0,1},{1,2},{2,3},{3,4},{4,5},{5,6},{6,7},{7,0},{8,9},{9,10},{10,1... | collective-permute-start | bytes 1572872 | tf_op jit(solution)/shard_map/ppermute | solution.py:112
  375.0 84.3 %collective-permute-start.6 = (bf16[4,1,32,2048]{3,2,0,1:T(8,128)(2,1)S(1)}, bf16[4,1,32,2048]{3,2,0,1:T(8,128)(2,1)S(1)}, u32[]{:S(2)}, u32[]{:S(2)}) collective-permute-start(bf16[4,1,32,2048]{3,2,0,1:T(8,128)(2,1)S(1)} %get-tuple-element.5), channel_id=1, source_target_pairs={{0,7},{1,0},{2,1},{3,2},{4,3},{5,4},{6,5},{7,6},{8,15},{9,8},{10,9... | collective-permute-start | bytes 1572872 | tf_op jit(solution)/shard_map/ppermute | solution.py:112
  375.9 82.5 %collective-permute-start.5 = (bf16[4,1,32,2048]{3,2,0,1:T(8,128)(2,1)S(1)}, bf16[4,1,32,2048]{3,2,0,1:T(8,128)(2,1)S(1)}, u32[]{:S(2)}, u32[]{:S(2)}) collective-permute-start(bf16[4,1,32,2048]{3,2,0,1:T(8,128)(2,1)S(1)} %get-tuple-element.6), channel_id=1, source_target_pairs={{0,6},{1,7},{2,0},{3,1},{4,2},{5,3},{6,4},{7,5},{8,14},{9,15},{10,... | collective-permute-start | bytes 1572872 | tf_op jit(solution)/shard_map/ppermute | solution.py:112
  375.9 81.6 %collective-permute-start.4 = (bf16[4,1,32,2048]{3,2,0,1:T(8,128)(2,1)S(1)}, bf16[4,1,32,2048]{3,2,0,1:T(8,128)(2,1)S(1)}, u32[]{:S(2)}, u32[]{:S(2)}) collective-permute-start(bf16[4,1,32,2048]{3,2,0,1:T(8,128)(2,1)S(1)} %get-tuple-element.7), channel_id=1, source_target_pairs={{0,5},{1,6},{2,7},{3,0},{4,1},{5,2},{6,3},{7,4},{8,13},{9,14},{10,... | collective-permute-start | bytes 1572872 | tf_op jit(solution)/shard_map/ppermute | solution.py:112
  376.0 44.8 %collective-permute-start.1 = (bf16[4,1,32,2048]{3,2,0,1:T(8,128)(2,1)S(1)}, bf16[4,1,32,2048]{3,2,0,1:T(8,128)(2,1)S(1)}, u32[]{:S(2)}, u32[]{:S(2)}) collective-permute-start(bf16[4,1,32,2048]{3,2,0,1:T(8,128)(2,1)S(1)} %get-tuple-element.10), channel_id=1, source_target_pairs={{0,2},{1,3},{2,4},{3,5},{4,6},{5,7},{6,0},{7,1},{8,10},{9,11},{10,... | collective-permute-start | bytes 1572872 | tf_op jit(solution)/shard_map/ppermute | solution.py:112
  391.4 57.9 %collective-permute-start.2 = (bf16[4,1,32,2048]{3,2,0,1:T(8,128)(2,1)S(1)}, bf16[4,1,32,2048]{3,2,0,1:T(8,128)(2,1)S(1)}, u32[]{:S(2)}, u32[]{:S(2)}) collective-permute-start(bf16[4,1,32,2048]{3,2,0,1:T(8,128)(2,1)S(1)} %get-tuple-element.9), channel_id=1, source_target_pairs={{0,3},{1,4},{2,5},{3,6},{4,7},{5,0},{6,1},{7,2},{8,11},{9,12},{10,... | collective-permute-start | bytes 1572872 | tf_op jit(solution)/shard_map/ppermute | solution.py:112
  420.8 35.9 %collective-permute-start.3 = (bf16[4,1,32,2048]{3,2,0,1:T(8,128)(2,1)S(1)}, bf16[4,1,32,2048]{3,2,0,1:T(8,128)(2,1)S(1)}, u32[]{:S(2)}, u32[]{:S(2)}) collective-permute-start(bf16[4,1,32,2048]{3,2,0,1:T(8,128)(2,1)S(1)} %get-tuple-element.8), channel_id=1, source_target_pairs={{0,4},{1,5},{2,6},{3,7},{4,0},{5,1},{6,2},{7,3},{8,12},{9,13},{10,... | collective-permute-start | bytes 1572872 | tf_op jit(solution)/shard_map/ppermute | solution.py:112
  469.8 9.8 %copy-start.1 = (bf16[64,2048]{1,0:T(8,128)(2,1)S(1)}, bf16[64,2048]{1,0:T(8,128)(2,1)}, u32[]{:S(2)}) copy-start(bf16[64,2048]{1,0:T(8,128)(2,1)} %param.11) | copy-start | bytes 786436
Sparse Core Ops, SparseCore 0:
  10.3 80.1 all-gather.1
